TPU v7x, 512 devices: a whole 4x4x16 slice. The times are simulated.
512 devices in a mesh: lat: 16 (over z_hi, y), lon: 32 (over z_lo, x, core).
Axes of the slice: x: 4, y: 4, z: 16 (z_hi: 4, z_lo: 4; z = z_hi * 4 + z_lo), core: 2. Of those that a mesh axis runs over, the one named last changes fastest.
Arguments:
- queries: float32 [64, 1024, 512], P('lat', 'lon'), may hold values from -80 to 80
- key_rows: float32 [512, 512], P(('lat', 'lon')), may hold values from -8 to 8
- value_rows: float32 [512, 512], P(('lat', 'lon')), may hold values from -6 to 6
- cotangent: float32 [64, 1024, 512], P('lat', 'lon'), may hold values from -25 to 25
- conv_taps: float32 [9, 512], replicated, may hold values from -1.75 to 1.75
Outputs:
- query_grad: float32 [64, 1024, 512], P('lat', 'lon')
- key_grad: float32 [512, 512], P(('lat', 'lon'))
- value_grad: float32 [512, 512], P(('lat', 'lon'))
- tap_update: float32 [9, 512], replicated
All inputs are finite; a program needn't handle non-finite values.
Results may differ from a plain program's by a relative error of at most 0.0003.
Values sent between devices are 32-bit elements; how exact they have to be, the bound alone decides.
A program may use at most 64 MiB of HBM per device.

v0:
```python
import jax
import jax.numpy as jnp
from jax import lax
from jax.sharding import PartitionSpec as P

HD = 64
HIGH = lax.Precision.HIGHEST
OFFSETS = ((-1, -1), (-1, 0), (-1, 1), (0, -1), (0, 0), (0, 1), (1, -1), (1, 0), (1, 1))


def joined_along(pieces, dim):
    lengths = list(pieces.shape[1:])
    lengths[dim] *= pieces.shape[0]
    return jnp.moveaxis(pieces, 0, dim).reshape(lengths)


def copy_for_each(value, axis):
    copies = jnp.broadcast_to(value, (lax.axis_size(axis), *value.shape))
    return lax.all_to_all(copies, axis, split_axis=0, concat_axis=0, tiled=True)


def gather_directly(value, axis, dim):
    return joined_along(copy_for_each(value, axis), dim)


def extended(value, sides, width):
    for axis, dim in sides:
        peers, length = (lax.axis_size(axis), value.shape[dim])
        up = [(i, (i + 1) % peers) for i in range(peers)]
        down = [(j, i) for i, j in up]
        last = lax.slice_in_dim(value, length - width, length, axis=dim)
        initial = lax.slice_in_dim(value, 0, width, axis=dim)
        before = lax.ppermute(last, axis, up)
        after = lax.ppermute(initial, axis, down)
        value = jnp.concatenate([before, value, after], axis=dim)
    return value


def cut_along(value, dim, peers):
    lengths = value.shape
    pieces = value.reshape(*lengths[:dim], peers, lengths[dim] // peers, *lengths[dim + 1 :])
    return jnp.moveaxis(pieces, dim, 0)


def summed_on_arrival(value, axis, dim):
    peers = lax.axis_size(axis)
    pieces = lax.all_to_all(cut_along(value, dim, peers), axis, 0, 0, tiled=True)
    return jnp.sum(pieces, axis=0)


def split_heads(matrix):
    return matrix.reshape(matrix.shape[0], -1, HD)


def latitude_weights(row_count, band_index, band_count):
    line_total = row_count * band_count
    centres = (jnp.arange(line_total, dtype=jnp.float32) + 0.5) * (jnp.pi / line_total)
    mean_cosine = jnp.sum(jnp.sin(centres)) / line_total
    mine = (band_index * row_count + jnp.arange(row_count, dtype=jnp.int32)).astype(jnp.float32)
    return jnp.sin((mine + 0.5) * (jnp.pi / line_total)) / mean_cosine


def close_poles(padded, row_dim, band_index, band_count):
    height = padded.shape[row_dim]
    positions = jnp.arange(height)
    outside = (positions == 0) & (band_index == 0) | (positions == height - 1) & (
        band_index == band_count - 1
    )
    shape_mask = [1] * padded.ndim
    shape_mask[row_dim] = height
    return jnp.where(outside.reshape(shape_mask), 0.0, padded)


def spread_taps(weighted, grad_padded, conv_taps):
    row_count, col_count = (weighted.shape[0], weighted.shape[1])
    result = weighted
    for tap_index, (shift_row, shift_col) in enumerate(OFFSETS):
        result = (
            result
            + conv_taps[tap_index]
            * grad_padded[
                1 - shift_row : 1 - shift_row + row_count, 1 - shift_col : 1 - shift_col + col_count
            ]
        )
    return result


def tap_terms(weighted, out_padded):
    row_count, col_count = (weighted.shape[0], weighted.shape[1])
    term_list = []
    for shift_row, shift_col in OFFSETS:
        term_list.append(
            jnp.sum(
                out_padded[
                    1 + shift_row : 1 + shift_row + row_count,
                    1 + shift_col : 1 + shift_col + col_count,
                ]
                * weighted,
                axis=(0, 1),
            )
        )
    return jnp.stack(term_list)


def group_logits(query_part, key_part):
    return jnp.einsum(
        "qhd,khd->hqk", split_heads(query_part), split_heads(key_part), precision=HIGH
    ) * HD ** (-0.5)


def body(queries, key_rows, value_rows, cotangent, conv_taps):
    row_count, col_count, channels = queries.shape
    band_count = lax.axis_size("lat")
    band_index = lax.axis_index("lat")
    weighted = cotangent * latitude_weights(row_count, band_index, band_count)[:, None, None]
    paired_rows = jnp.concatenate([key_rows, value_rows], 1)
    paired_sector = gather_directly(paired_rows, "lon", 0)
    paired_all = lax.all_gather(paired_sector, "lat", axis=0, tiled=True)
    key_all = paired_all[:, :channels]
    value_all = paired_all[:, channels:]
    token_count = row_count * col_count
    key_count = key_all.shape[0]
    query_flat = queries.reshape(token_count, channels)
    group_width = 2 * HD
    group_count = channels // group_width
    outputs = []
    peaks = []
    sums_soft = []
    for group_index in range(group_count):
        col_start = group_index * group_width
        col_stop = col_start + group_width
        logits = group_logits(query_flat[:, col_start:col_stop], key_all[:, col_start:col_stop])
        row_peak = jnp.max(logits, -1, keepdims=True)
        raised = jnp.exp(logits - row_peak)
        normaliser = jnp.sum(raised, -1, keepdims=True)
        soft_weights = raised / normaliser
        outputs.append(
            jnp.einsum(
                "hqk,khd->qhd",
                soft_weights,
                split_heads(value_all[:, col_start:col_stop]),
                precision=HIGH,
            ).reshape(token_count, group_width)
        )
        peaks.append(row_peak)
        sums_soft.append(normaliser)
    out_flat = jnp.concatenate(outputs, 1)
    out_grid = out_flat.reshape(row_count, col_count, channels)
    both_padded = close_poles(
        extended(jnp.stack([weighted, out_grid]), (("lat", 1), ("lon", 2)), 1),
        1,
        band_index,
        band_count,
    )
    grad_padded = both_padded[0]
    out_padded = both_padded[1]
    out_grad = spread_taps(weighted, grad_padded, conv_taps)
    tap_sum = lax.psum(tap_terms(weighted, out_padded), ("lat", "lon"))
    tap_update = tap_sum / jnp.sqrt(jnp.mean(tap_sum * tap_sum) + 1e-06)
    grad_flat = out_grad.reshape(token_count, channels)
    query_parts = []
    key_parts = []
    value_parts = []
    for group_index in range(group_count):
        col_start = group_index * group_width
        col_stop = col_start + group_width
        query_heads = split_heads(query_flat[:, col_start:col_stop])
        key_heads = split_heads(key_all[:, col_start:col_stop])
        logits = jnp.einsum("qhd,khd->hqk", query_heads, key_heads, precision=HIGH) * HD ** (-0.5)
        soft_weights = jnp.exp(logits - peaks[group_index]) / sums_soft[group_index]
        grad_heads = split_heads(grad_flat[:, col_start:col_stop])
        value_parts.append(
            jnp.einsum("hqk,qhd->khd", soft_weights, grad_heads, precision=HIGH).reshape(
                key_count, group_width
            )
        )
        prob_grad = jnp.einsum(
            "qhd,khd->hqk",
            grad_heads,
            split_heads(value_all[:, col_start:col_stop]),
            precision=HIGH,
        )
        row_dot = jnp.transpose(
            jnp.sum(grad_heads * split_heads(out_flat[:, col_start:col_stop]), -1)
        )[:, :, None]
        logit_grad = soft_weights * (prob_grad - row_dot)
        query_parts.append(
            (
                jnp.einsum("hqk,khd->qhd", logit_grad, key_heads, precision=HIGH) * HD ** (-0.5)
            ).reshape(token_count, group_width)
        )
        key_parts.append(
            (
                jnp.einsum("hqk,qhd->khd", logit_grad, query_heads, precision=HIGH) * HD ** (-0.5)
            ).reshape(key_count, group_width)
        )
    paired_terms = jnp.concatenate(key_parts + value_parts, 1)
    paired_band = lax.psum_scatter(paired_terms, "lat", scatter_dimension=0, tiled=True)
    paired_grad = summed_on_arrival(paired_band, "lon", 0)
    key_grad = paired_grad[:, :channels]
    value_grad = paired_grad[:, channels:]
    query_grad = jnp.concatenate(query_parts, 1).reshape(row_count, col_count, channels)
    return (query_grad, key_grad, value_grad, tap_update)


def solution(mesh):
    placed = (
        P("lat", "lon", None),
        P(("lat", "lon"), None),
        P(("lat", "lon"), None),
        P("lat", "lon", None),
        P(),
    )
    return jax.shard_map(
        body,
        mesh=mesh,
        in_specs=placed,
        out_specs=(P("lat", "lon", None), P(("lat", "lon"), None), P(("lat", "lon"), None), P()),
        check_vma=False,
    )
```

profile of v0, /device:TPU:1, one launch (start us, length us, event | category | flops | bytes accessed | tf_op | source)
XLA Modules:
  0.0 343.2 jit_solution(12765066276765064027)
XLA Ops:
  7.2 0.7 pad_maximum_fusion.13
  8.0 18.8 %all_to_all.10 = f32[32,1,1024]{2,1,0:T(1,128)} all-to-all(f32[32,1,1024]{2,1,0:T(1,128)S(1)} %broadcast_in_dim.10), channel_id=1, replica_groups=mesh['lat'=16,'lon'=32] {'lon'}, dimensions={0} | all-to-all | bytes 262144 | tf_op jit(solution)/shard_map/all_to_all | solution.py:19
  26.9 1.0 fusion.53
  27.9 0.7 copy.151
  28.6 0.7 copy.150
  29.5 0.7 sine_reduce_fusion
  30.8 1.0 fusion.50
  31.8 88.1 %all-gather.3.cloned.1.call-done = f32[512,1,1024]{2,1,0:T(1,128)} async-done(((f32[32,1,1024]{2,1,0:T(1,128)}), f32[512,1,1024]{2,1,0:T(1,128)}) %all-gather.3.cloned.1.call-update) | async-done | bytes 2097168 | tf_op jit(solution)/shard_map/all_gather | solution.py:118
  120.0 2.1 copy.158
  122.8 0.8 copy.91
  123.9 0.9 copy.83
  124.8 1.0 fusion.56
  125.9 0.5 convolution_bitcast_fusion
  126.7 1.0 fusion.58
  127.8 1.1 convolution_bitcast_fusion.2
  128.9 1.0 copy.90
  130.0 1.0 fusion.57
  131.2 0.5 convolution_bitcast_fusion.1
  131.9 1.0 fusion.59
  133.1 1.4 convolution_bitcast_fusion.3
  134.8 2.1 collective-permute-start
  136.9 9.2 %collective-permute-start.1 = (f32[2,1,32,512]{3,2,1,0:T(8,128)S(1)}, f32[2,1,32,512]{3,2,1,0:T(8,128)S(1)}, u32[]{:S(2)}, u32[]{:S(2)}) collective-permute-start(f32[2,1,32,512]{3,2,1,0:T(8,128)S(1)} %get-tuple-element.26), channel_id=1, source_target_pairs={{32,0},{64,32},{96,64},{128,96},{160,128},{192,160},{224,192},{256... | collective-permute-start | bytes 393224 | tf_op jit(solution)/shard_map/ppermute | solution.py:34
  146.1 4.7 %collective-permute-done = f32[2,1,32,512]{3,2,1,0:T(8,128)S(1)} collective-permute-done((f32[2,1,32,512]{3,2,1,0:T(8,128)S(1)}, f32[2,1,32,512]{3,2,1,0:T(8,128)S(1)}, u32[]{:S(2)}, u32[]{:S(2)}) %collective-permute-start) | collective-permute-done | bytes 131104 | tf_op jit(solution)/shard_map/ppermute | solution.py:33
  150.9 3.2 collective-permute-start.2
  154.1 2.1 collective-permute-start.3
  156.3 3.3 collective-permute-done.3
  159.9 0.3 fusion.29
  160.2 0.7 fusion.52
  160.9 1.6 copy.153
  162.4 0.9 multiply_reduce_fusion.3
  163.3 1.6 copy.155
  164.9 0.9 multiply_reduce_fusion.1
  165.8 1.6 copy.154
  167.3 0.9 multiply_reduce_fusion.2
  168.2 1.6 copy.156
  169.8 0.9 multiply_reduce_fusion
  170.8 1.6 fusion.38
  172.4 1.0 fusion
  173.4 0.7 convolution_multiply_fusion.4
  174.1 0.7 fusion.44
  174.9 1.0 fusion.2
  175.9 0.7 convolution_multiply_fusion.6
  176.6 0.7 fusion.41
  177.4 1.0 fusion.1
  178.4 0.7 convolution_multiply_fusion.5
  179.1 0.7 fusion.47
  179.9 1.0 fusion.3
  180.9 0.7 convolution_multiply_fusion.7
  181.8 1.9 copy.146
  183.8 0.3 fusion.20
  184.1 117.4 %psum.7 = f32[9,512]{1,0:T(8,128)S(1)} all-reduce(f32[9,512]{1,0:T(8,128)S(1)} %stack.47), channel_id=1, replica_groups=mesh['lat'=16,'lon'=32] {'lat','lon'}, use_global_device_ids=true, to_apply=%region_24.25 | all-reduce | flops 4608 | bytes 36864 | tf_op jit(solution)/shard_map/psum | solution.py:158
  301.5 0.6 multiply_reduce_fusion.4
  302.8 0.4 fusion.8
  303.5 0.4 fusion.10
  304.2 0.4 fusion.9
  304.9 13.6 %reduce-scatter.4.cloned.1.call-done = f32[32,1024]{1,0:T(8,128)} async-done(((f32[512,1024]{1,0:T(8,128)}), f32[32,1024]{1,0:T(8,128)}) %reduce-scatter.4.cloned.1.call-update) | async-done | bytes 131088
  318.5 1.1 copy.147
  319.6 0.8 copy.125
  320.4 6.7 %all-to-all-start.1 = ((f32[32,1,1024]{2,1,0:T(1,128)}), f32[32,1,1024]{2,1,0:T(1,128)S(1)}, u32[]{:S(2)}, u32[]{:S(2)}) async-start(f32[32,1,1024]{2,1,0:T(1,128)} %copy.125), calls=%async_computation.1 | async-start | bytes 262144 | tf_op jit(solution)/shard_map/all_to_all | solution.py:47
  327.1 0.4 fusion.11
  327.8 0.7 pad_maximum_fusion
  328.5 0.6 broadcast_divide_fusion
  329.2 6.5 %all-to-all-done.1 = f32[32,1,1024]{2,1,0:T(1,128)S(1)} async-done(((f32[32,1,1024]{2,1,0:T(1,128)}), f32[32,1,1024]{2,1,0:T(1,128)S(1)}, u32[]{:S(2)}, u32[]{:S(2)}) %all-to-all-start.1) | async-done | bytes 131104 | tf_op jit(solution)/shard_map/all_to_all | solution.py:47
  335.7 0.6 fusion.55
  (122 shorter events, 4.4 us)
Async XLA Ops:
  7.2 112.8 %all-gather.3.cloned.1.call-start = ((), (), s32[]{:S(2)}) async-start(), calls=%async_computation.3 | async-start | bytes 2228224 | tf_op jit(solution)/shard_map/all_gather | solution.py:118
  26.8 291.7 %reduce-scatter.4.cloned.1.call-start = ((), (), s32[]{:S(2)}) async-start(), calls=%async_computation.4 | async-start | bytes 2228224
  29.4 95.3 %copy-start.17 = (f32[128,128]{0,1:T(8,128)}, f32[128,128]{0,1:T(8,128)S(1)}, u32[]{:S(2)}) copy-start(f32[128,128]{0,1:T(8,128)S(1)} %copy.152) | copy-start | bytes 196612
  122.5 3.4 copy-start.1
  122.6 3.8 %copy-start.28 = (f32[512,128]{0,1:T(8,128)}, f32[512,128]{0,1:T(8,128)S(1)}, u32[]{:S(2)}) copy-start(f32[512,128]{0,1:T(8,128)S(1)} %copy.96) | copy-start | bytes 786436
  123.8 2.9 copy-start.3
  123.9 3.9 %copy-start.26 = (f32[512,128]{0,1:T(8,128)}, f32[512,128]{0,1:T(8,128)S(1)}, u32[]{:S(2)}) copy-start(f32[512,128]{0,1:T(8,128)S(1)} %copy.86) | copy-start | bytes 786436
  123.9 2.8 copy-start.15
  126.4 3.6 %copy-start.19 = (f32[128,2,64]{0,2,1:T(8,128)}, f32[128,2,64]{0,2,1:T(8,128)S(1)}, u32[]{:S(2)}) copy-start(f32[128,2,64]{0,2,1:T(8,128)S(1)} %convolution_bitcast_fusion) | copy-start | bytes 196612
  126.4 3.6 %copy-start.13 = (f32[128,128]{0,1:T(8,128)S(1)}, f32[128,128]{0,1:T(8,128)}, u32[]{:S(2)}) copy-start(f32[128,128]{0,1:T(8,128)} %copy.151) | copy-start | bytes 196612
  127.7 3.4 %copy-start.24 = (f32[512,128]{0,1:T(8,128)S(1)}, f32[512,128]{0,1:T(8,128)}, u32[]{:S(2)}) copy-start(f32[512,128]{0,1:T(8,128)} %copy.91) | copy-start | bytes 786436
  131.7 19.2 %copy-start.21 = (f32[128,2,64]{0,2,1:T(8,128)}, f32[128,2,64]{0,2,1:T(8,128)S(1)}, u32[]{:S(2)}) copy-start(f32[128,2,64]{0,2,1:T(8,128)S(1)} %convolution_bitcast_fusion.1) | copy-start | bytes 196612
  132.9 13.2 %copy-start.34 = (f32[9,512]{1,0:T(8,128)S(1)}, f32[9,512]{1,0:T(8,128)}, u32[]{:S(2)}) copy-start(f32[9,512]{1,0:T(8,128)} %param.9) | copy-start | bytes 55300
  134.5 16.3 %copy-start.22 = (f32[128,2,64]{0,2,1:T(8,128)}, f32[128,2,64]{0,2,1:T(8,128)S(1)}, u32[]{:S(2)}) copy-start(f32[128,2,64]{0,2,1:T(8,128)S(1)} %convolution_bitcast_fusion.3) | copy-start | bytes 196612
  134.8 16.0 %collective-permute-start = (f32[2,1,32,512]{3,2,1,0:T(8,128)S(1)}, f32[2,1,32,512]{3,2,1,0:T(8,128)S(1)}, u32[]{:S(2)}, u32[]{:S(2)}) collective-permute-start(f32[2,1,32,512]{3,2,1,0:T(8,128)S(1)} %get-tuple-element.25), channel_id=1, source_target_pairs={{0,32},{32,64},{64,96},{96,128},{128,160},{160,192},{192,224},{224... | collective-permute-start | bytes 393224 | tf_op jit(solution)/shard_map/ppermute | solution.py:33
  136.9 13.9 %collective-permute-start.1 = (f32[2,1,32,512]{3,2,1,0:T(8,128)S(1)}, f32[2,1,32,512]{3,2,1,0:T(8,128)S(1)}, u32[]{:S(2)}, u32[]{:S(2)}) collective-permute-start(f32[2,1,32,512]{3,2,1,0:T(8,128)S(1)} %get-tuple-element.26), channel_id=1, source_target_pairs={{32,0},{64,32},{96,64},{128,96},{160,128},{192,160},{224,192},{256... | collective-permute-start | bytes 393224 | tf_op jit(solution)/shard_map/ppermute | solution.py:34
  150.9 9.0 %copy-start = (f32[4,32,512]{2,1,0:T(8,128)S(1)}, f32[4,32,512]{2,1,0:T(8,128)}, u32[]{:S(2)}) copy-start(f32[4,32,512]{2,1,0:T(8,128)} %param.8) | copy-start | bytes 786436
  150.9 5.4 %collective-permute-start.2 = (f32[2,6,1,512]{3,2,1,0:T(1,128)S(1)}, f32[2,6,1,512]{3,2,1,0:T(1,128)S(1)}, u32[]{:S(2)}, u32[]{:S(2)}) collective-permute-start(f32[2,6,1,512]{3,2,1,0:T(1,128)S(1)} %get-tuple-element.23), channel_id=1, source_target_pairs={{0,1},{1,2},{2,3},{3,4},{4,5},{5,6},{6,7},{7,8},{8,9},{9,10},{10,1... | collective-permute-start | bytes 73736 | tf_op jit(solution)/shard_map/ppermute | solution.py:33
  154.1 5.4 %collective-permute-start.3 = (f32[2,6,1,512]{3,2,1,0:T(1,128)S(1)}, f32[2,6,1,512]{3,2,1,0:T(1,128)S(1)}, u32[]{:S(2)}, u32[]{:S(2)}) collective-permute-start(f32[2,6,1,512]{3,2,1,0:T(1,128)S(1)} %get-tuple-element.24), channel_id=1, source_target_pairs={{1,0},{2,1},{3,2},{4,3},{5,4},{6,5},{7,6},{8,7},{9,8},{10,9},{11,1... | collective-permute-start | bytes 73736 | tf_op jit(solution)/shard_map/ppermute | solution.py:34
  159.9 9.9 %copy-start.20 = (f32[128,2,64]{0,2,1:T(8,128)S(1)}, f32[128,2,64]{0,2,1:T(8,128)}, u32[]{:S(2)}) copy-start(f32[128,2,64]{0,2,1:T(8,128)} %copy-done.19) | copy-start | bytes 196612
  169.8 2.5 copy-start.29
  169.8 2.5 copy-start.33
  170.7 2.6 copy-start.18
  170.7 3.4 copy-start.32
  172.4 2.5 copy-start.27
  173.4 2.5 copy-start.7
  174.1 1.8 copy-start.16
  174.1 2.5 copy-start.31
  174.8 2.5 copy-start.25
  175.9 2.5 copy-start.9
  176.6 1.8 copy-start.14
  176.6 2.5 copy-start.30
  177.4 2.5 copy-start.23
  178.4 1.4 copy-start.11
  180.9 0.9 copy-start.5
  183.7 119.1 %copy-start.2 = (f32[512,128]{0,1:T(8,128)S(1)}, f32[512,128]{0,1:T(8,128)}, u32[]{:S(2)}) copy-start(f32[512,128]{0,1:T(8,128)} %copy-done.1) | copy-start | bytes 786436
  183.7 119.1 %copy-start.8 = (f32[2,128,512]{1,2,0:T(8,128)S(1)}, f32[2,128,512]{1,2,0:T(8,128)}, u32[]{:S(2)}) copy-start(f32[2,128,512]{1,2,0:T(8,128)} %copy-done.7) | copy-start | bytes 1572868
  183.7 119.8 %copy-start.4 = (f32[512,128]{0,1:T(8,128)S(1)}, f32[512,128]{0,1:T(8,128)}, u32[]{:S(2)}) copy-start(f32[512,128]{0,1:T(8,128)} %copy-done.3) | copy-start | bytes 786436
  183.7 119.8 %copy-start.10 = (f32[2,128,512]{1,2,0:T(8,128)S(1)}, f32[2,128,512]{1,2,0:T(8,128)}, u32[]{:S(2)}) copy-start(f32[2,128,512]{1,2,0:T(8,128)} %copy-done.9) | copy-start | bytes 1572868
  183.7 120.5 %copy-start.12 = (f32[2,128,512]{1,2,0:T(8,128)S(1)}, f32[2,128,512]{1,2,0:T(8,128)}, u32[]{:S(2)}) copy-start(f32[2,128,512]{1,2,0:T(8,128)} %copy-done.11) | copy-start | bytes 1572868
  303.4 23.7 %copy-start.6 = (f32[2,128,512]{1,2,0:T(8,128)S(1)}, f32[2,128,512]{1,2,0:T(8,128)}, u32[]{:S(2)}) copy-start(f32[2,128,512]{1,2,0:T(8,128)} %copy-done.5) | copy-start | bytes 1572868
  320.4 15.2 %all-to-all-start.1 = ((f32[32,1,1024]{2,1,0:T(1,128)}), f32[32,1,1024]{2,1,0:T(1,128)S(1)}, u32[]{:S(2)}, u32[]{:S(2)}) async-start(f32[32,1,1024]{2,1,0:T(1,128)} %copy.125), calls=%async_computation.1 | async-start | bytes 262144 | tf_op jit(solution)/shard_map/all_to_all | solution.py:47
Sparse Core Ops, SparseCore 0:
  26.9 93.0 all-gather.2
  183.8 134.6 reduce-scatter.3
where the time goes:
time: 344 us; the launch traced here: 343 us
  blocking collectives  136 us (40%)
  waiting for transfers between devices  116 us (34%)
  starting transfers between devices  23.4 us (7%)
  local copies, waits for them, and re-layouts  21.9 us (6%)
  matrix products  19.9 us (6%)
  between operations  16.2 us (5%)
  other arithmetic  9.35 us (3%)
    psum x1, blocking collectives, body(): tap_sum = lax.psum(tap_terms(weighted, out_padded), ('lat', 'lon'))  117 us
    all_gather x1, waiting for transfers between devices, body(): paired_all = lax.all_gather(paired_sector, 'lat', axis=0, tiled=True)  88.1 us
    all_to_all x1, blocking collectives, copy_for_each(): return lax.all_to_all(copies, axis, split_axis=0, concat_axis=0, tiled=True)  18.8 us
    unnamed x3, waiting for transfers between devices  13.6 us
    unnamed x88, local copies, waits for them, and re-layouts  13.2 us
    ppermute x2, starting transfers between devices, extended(): after = lax.ppermute(initial, axis, down)  11.3 us
  transfers between devices with their start and end apart: 7, of which 5 were waited for; matrix products, arithmetic and copies ran while one was open for 3% of the time, Pallas kernels for 0%

commit v1 on v0

--- a/solution.py
+++ b/solution.py
@@ -155,7 +155,13 @@
     grad_padded = both_padded[0]
     out_padded = both_padded[1]
     out_grad = spread_taps(weighted, grad_padded, conv_taps)
-    tap_sum = lax.psum(tap_terms(weighted, out_padded), ("lat", "lon"))
+
+    def match_the_thing(original):
+        for ix in ("lon", "lat"):
+            original = lax.psum(original, axis_name=ix)
+        return original
+
+    tap_sum = match_the_thing(tap_terms(weighted, out_padded))
     tap_update = tap_sum / jnp.sqrt(jnp.mean(tap_sum * tap_sum) + 1e-06)
     grad_flat = out_grad.reshape(token_count, channels)
     query_parts = []

time: 344 us -> 454 us (1.32)
  blocking collectives: 136 us -> 243 us
  starting transfers between devices: 23.4 us -> 40.2 us
  waiting for transfers between devices: 116 us -> 103 us
    psum x1 -> x2, blocking collectives: 117 us -> 224 us  [match_the_thing(): original = lax.psum(original, axis_name=ix)]
    all_to_all x1, starting transfers between devices: 6.68 us -> 23.5 us  [summed_on_arrival(): lax.all_to_all(cut_along(value, dim, peers), axis, 0, 0, tiled=True)]
    unnamed x3, waiting for transfers between devices: 13.6 us -> 0.04 us
  transfers between devices with their start and end apart: 7 -> 7, of which waited for: 5 -> 4; matrix products, arithmetic and copies ran while one was open for 3% -> 2% of each run, Pallas kernels for 0% -> 0%
where the time goes in v1:
time: 454 us; the launch traced here: 453 us
  blocking collectives  243 us (54%)
  waiting for transfers between devices  103 us (23%)
  starting transfers between devices  40.2 us (9%)
  local copies, waits for them, and re-layouts  21.9 us (5%)
  matrix products  19.9 us (4%)
  between operations  16.2 us (4%)
  other arithmetic  9.35 us (2%)
    psum x2, blocking collectives, match_the_thing(): original = lax.psum(original, axis_name=ix)  224 us
    all_gather x1, waiting for transfers between devices, body(): paired_all = lax.all_gather(paired_sector, 'lat', axis=0, tiled=True)  88.1 us
    all_to_all x1, starting transfers between devices, summed_on_arrival(): lax.all_to_all(cut_along(value, dim, peers), axis, 0, 0, tiled=True)  23.5 us
    all_to_all x1, blocking collectives, copy_for_each(): return lax.all_to_all(copies, axis, split_axis=0, concat_axis=0, tiled=True)  18.8 us
    unnamed x88, local copies, waits for them, and re-layouts  13.2 us
    ppermute x2, starting transfers between devices, extended(): after = lax.ppermute(initial, axis, down)  11.3 us
  transfers between devices with their start and end apart: 7, of which 4 were waited for; matrix products, arithmetic and copies ran while one was open for 2% of the time, Pallas kernels for 0%

profile of v1, /device:TPU:1, one launch (start us, length us, event | category | flops | bytes accessed | tf_op | source)
XLA Modules:
  0.0 453.0 jit_solution(11724858027187844671)
XLA Ops:
  7.2 0.7 pad_maximum_fusion.13
  8.0 18.8 %all_to_all.10 = f32[32,1,1024]{2,1,0:T(1,128)} all-to-all(f32[32,1,1024]{2,1,0:T(1,128)S(1)} %broadcast_in_dim.10), channel_id=1, replica_groups=mesh['lat'=16,'lon'=32] {'lon'}, dimensions={0} | all-to-all | bytes 262144 | tf_op jit(solution)/shard_map/all_to_all | solution.py:19
  26.9 1.0 fusion.53
  27.9 0.7 copy.151
  28.6 0.7 copy.150
  29.5 0.7 sine_reduce_fusion
  30.8 1.0 fusion.50
  31.8 88.1 %all-gather.3.cloned.1.call-done = f32[512,1,1024]{2,1,0:T(1,128)} async-done(((f32[32,1,1024]{2,1,0:T(1,128)}), f32[512,1,1024]{2,1,0:T(1,128)}) %all-gather.3.cloned.1.call-update) | async-done | bytes 2097168 | tf_op jit(solution)/shard_map/all_gather | solution.py:118
  120.0 2.1 copy.158
  122.8 0.8 copy.91
  123.9 0.9 copy.83
  124.8 1.0 fusion.56
  125.9 0.5 convolution_bitcast_fusion
  126.7 1.0 fusion.58
  127.8 1.1 convolution_bitcast_fusion.2
  128.9 1.0 copy.90
  130.0 1.0 fusion.57
  131.2 0.5 convolution_bitcast_fusion.1
  131.9 1.0 fusion.59
  133.1 1.4 convolution_bitcast_fusion.3
  134.8 2.1 collective-permute-start
  136.9 9.2 %collective-permute-start.1 = (f32[2,1,32,512]{3,2,1,0:T(8,128)S(1)}, f32[2,1,32,512]{3,2,1,0:T(8,128)S(1)}, u32[]{:S(2)}, u32[]{:S(2)}) collective-permute-start(f32[2,1,32,512]{3,2,1,0:T(8,128)S(1)} %get-tuple-element.26), channel_id=1, source_target_pairs={{32,0},{64,32},{96,64},{128,96},{160,128},{192,160},{224,192},{256... | collective-permute-start | bytes 393224 | tf_op jit(solution)/shard_map/ppermute | solution.py:34
  146.1 4.7 %collective-permute-done = f32[2,1,32,512]{3,2,1,0:T(8,128)S(1)} collective-permute-done((f32[2,1,32,512]{3,2,1,0:T(8,128)S(1)}, f32[2,1,32,512]{3,2,1,0:T(8,128)S(1)}, u32[]{:S(2)}, u32[]{:S(2)}) %collective-permute-start) | collective-permute-done | bytes 131104 | tf_op jit(solution)/shard_map/ppermute | solution.py:33
  150.9 3.2 collective-permute-start.2
  154.1 2.1 collective-permute-start.3
  156.3 3.3 collective-permute-done.3
  159.9 0.3 fusion.29
  160.2 0.7 fusion.52
  160.9 1.6 copy.153
  162.4 0.9 multiply_reduce_fusion.3
  163.3 1.6 copy.155
  164.9 0.9 multiply_reduce_fusion.1
  165.8 1.6 copy.154
  167.3 0.9 multiply_reduce_fusion.2
  168.2 1.6 copy.156
  169.8 0.9 multiply_reduce_fusion
  170.8 1.6 fusion.38
  172.4 1.0 fusion
  173.4 0.7 convolution_multiply_fusion.4
  174.1 0.7 fusion.44
  174.9 1.0 fusion.2
  175.9 0.7 convolution_multiply_fusion.6
  176.6 0.7 fusion.41
  177.4 1.0 fusion.1
  178.4 0.7 convolution_multiply_fusion.5
  179.1 0.7 fusion.47
  179.9 1.0 fusion.3
  180.9 0.7 convolution_multiply_fusion.7
  181.8 1.9 copy.146
  183.8 0.3 fusion.20
  184.1 137.3 %psum.14 = f32[9,512]{1,0:T(8,128)S(1)} all-reduce(f32[9,512]{1,0:T(8,128)S(1)} %stack.47), channel_id=1, replica_groups=mesh['lat'=16,'lon'=32] {'lon'}, use_global_device_ids=true, to_apply=%region_24.25 | all-reduce | flops 4608 | bytes 36864 | tf_op jit(solution)/shard_map/psum | solution.py:161
  321.4 86.6 %psum.15 = f32[9,512]{1,0:T(8,128)S(1)} all-reduce(f32[9,512]{1,0:T(8,128)S(1)} %psum.14), channel_id=1, replica_groups=mesh['lat'=16,'lon'=32] {'lat'}, use_global_device_ids=true, to_apply=%region_25.26 | all-reduce | flops 4608 | bytes 36864 | tf_op jit(solution)/shard_map/psum | solution.py:161
  408.0 0.6 multiply_reduce_fusion.4
  409.4 0.4 fusion.8
  410.1 0.4 fusion.10
  410.8 0.4 fusion.9
  411.5 1.1 copy.147
  412.6 0.8 copy.125
  413.4 23.5 %all-to-all-start.1 = ((f32[32,1,1024]{2,1,0:T(1,128)}), f32[32,1,1024]{2,1,0:T(1,128)S(1)}, u32[]{:S(2)}, u32[]{:S(2)}) async-start(f32[32,1,1024]{2,1,0:T(1,128)} %copy.125), calls=%async_computation.1 | async-start | bytes 262144 | tf_op jit(solution)/shard_map/all_to_all | solution.py:47
  436.9 0.4 fusion.11
  437.6 0.7 pad_maximum_fusion
  438.3 0.6 broadcast_divide_fusion
  438.9 6.6 %all-to-all-done.1 = f32[32,1,1024]{2,1,0:T(1,128)S(1)} async-done(((f32[32,1,1024]{2,1,0:T(1,128)}), f32[32,1,1024]{2,1,0:T(1,128)S(1)}, u32[]{:S(2)}, u32[]{:S(2)}) %all-to-all-start.1) | async-done | bytes 131104 | tf_op jit(solution)/shard_map/all_to_all | solution.py:47
  445.6 0.6 fusion.55
  (123 shorter events, 4.4 us)
Async XLA Ops:
  7.2 112.8 %all-gather.3.cloned.1.call-start = ((), (), s32[]{:S(2)}) async-start(), calls=%async_computation.3 | async-start | bytes 2228224 | tf_op jit(solution)/shard_map/all_gather | solution.py:118
  26.8 384.6 %reduce-scatter.4.cloned.1.call-start = ((), (), s32[]{:S(2)}) async-start(), calls=%async_computation.4 | async-start | bytes 2228224
  29.4 95.3 %copy-start.17 = (f32[128,128]{0,1:T(8,128)}, f32[128,128]{0,1:T(8,128)S(1)}, u32[]{:S(2)}) copy-start(f32[128,128]{0,1:T(8,128)S(1)} %copy.152) | copy-start | bytes 196612
  122.5 3.4 copy-start.1
  122.6 3.8 copy-start.28
  123.8 2.9 copy-start.3
  123.9 3.9 copy-start.26
  123.9 2.8 copy-start.15
  126.4 3.6 copy-start.19
  126.4 3.6 copy-start.13
  127.7 3.4 copy-start.24
  131.7 19.2 %copy-start.21 = (f32[128,2,64]{0,2,1:T(8,128)}, f32[128,2,64]{0,2,1:T(8,128)S(1)}, u32[]{:S(2)}) copy-start(f32[128,2,64]{0,2,1:T(8,128)S(1)} %convolution_bitcast_fusion.1) | copy-start | bytes 196612
  132.9 13.2 %copy-start.34 = (f32[9,512]{1,0:T(8,128)S(1)}, f32[9,512]{1,0:T(8,128)}, u32[]{:S(2)}) copy-start(f32[9,512]{1,0:T(8,128)} %param.9) | copy-start | bytes 55300
  134.5 16.3 %copy-start.22 = (f32[128,2,64]{0,2,1:T(8,128)}, f32[128,2,64]{0,2,1:T(8,128)S(1)}, u32[]{:S(2)}) copy-start(f32[128,2,64]{0,2,1:T(8,128)S(1)} %convolution_bitcast_fusion.3) | copy-start | bytes 196612
  134.8 16.0 %collective-permute-start = (f32[2,1,32,512]{3,2,1,0:T(8,128)S(1)}, f32[2,1,32,512]{3,2,1,0:T(8,128)S(1)}, u32[]{:S(2)}, u32[]{:S(2)}) collective-permute-start(f32[2,1,32,512]{3,2,1,0:T(8,128)S(1)} %get-tuple-element.25), channel_id=1, source_target_pairs={{0,32},{32,64},{64,96},{96,128},{128,160},{160,192},{192,224},{224... | collective-permute-start | bytes 393224 | tf_op jit(solution)/shard_map/ppermute | solution.py:33
  136.9 13.9 %collective-permute-start.1 = (f32[2,1,32,512]{3,2,1,0:T(8,128)S(1)}, f32[2,1,32,512]{3,2,1,0:T(8,128)S(1)}, u32[]{:S(2)}, u32[]{:S(2)}) collective-permute-start(f32[2,1,32,512]{3,2,1,0:T(8,128)S(1)} %get-tuple-element.26), channel_id=1, source_target_pairs={{32,0},{64,32},{96,64},{128,96},{160,128},{192,160},{224,192},{256... | collective-permute-start | bytes 393224 | tf_op jit(solution)/shard_map/ppermute | solution.py:34
  150.9 9.0 %copy-start = (f32[4,32,512]{2,1,0:T(8,128)S(1)}, f32[4,32,512]{2,1,0:T(8,128)}, u32[]{:S(2)}) copy-start(f32[4,32,512]{2,1,0:T(8,128)} %param.8) | copy-start | bytes 786436
  150.9 5.4 %collective-permute-start.2 = (f32[2,6,1,512]{3,2,1,0:T(1,128)S(1)}, f32[2,6,1,512]{3,2,1,0:T(1,128)S(1)}, u32[]{:S(2)}, u32[]{:S(2)}) collective-permute-start(f32[2,6,1,512]{3,2,1,0:T(1,128)S(1)} %get-tuple-element.23), channel_id=1, source_target_pairs={{0,1},{1,2},{2,3},{3,4},{4,5},{5,6},{6,7},{7,8},{8,9},{9,10},{10,1... | collective-permute-start | bytes 73736 | tf_op jit(solution)/shard_map/ppermute | solution.py:33
  154.1 5.4 %collective-permute-start.3 = (f32[2,6,1,512]{3,2,1,0:T(1,128)S(1)}, f32[2,6,1,512]{3,2,1,0:T(1,128)S(1)}, u32[]{:S(2)}, u32[]{:S(2)}) collective-permute-start(f32[2,6,1,512]{3,2,1,0:T(1,128)S(1)} %get-tuple-element.24), channel_id=1, source_target_pairs={{1,0},{2,1},{3,2},{4,3},{5,4},{6,5},{7,6},{8,7},{9,8},{10,9},{11,1... | collective-permute-start | bytes 73736 | tf_op jit(solution)/shard_map/ppermute | solution.py:34
  159.9 9.9 %copy-start.20 = (f32[128,2,64]{0,2,1:T(8,128)S(1)}, f32[128,2,64]{0,2,1:T(8,128)}, u32[]{:S(2)}) copy-start(f32[128,2,64]{0,2,1:T(8,128)} %copy-done.19) | copy-start | bytes 196612
  169.8 2.5 copy-start.29
  169.8 2.5 copy-start.33
  170.7 2.6 copy-start.18
  170.7 3.4 copy-start.32
  172.4 2.5 copy-start.27
  173.4 2.5 copy-start.7
  174.1 1.8 copy-start.16
  174.1 2.5 copy-start.31
  174.8 2.5 copy-start.25
  175.9 2.5 copy-start.9
  176.6 1.8 copy-start.14
  176.6 2.5 copy-start.30
  177.4 2.5 copy-start.23
  178.4 1.4 copy-start.11
  180.9 0.9 copy-start.5
  183.7 225.6 %copy-start.2 = (f32[512,128]{0,1:T(8,128)S(1)}, f32[512,128]{0,1:T(8,128)}, u32[]{:S(2)}) copy-start(f32[512,128]{0,1:T(8,128)} %copy-done.1) | copy-start | bytes 786436
  183.7 225.7 %copy-start.8 = (f32[2,128,512]{1,2,0:T(8,128)S(1)}, f32[2,128,512]{1,2,0:T(8,128)}, u32[]{:S(2)}) copy-start(f32[2,128,512]{1,2,0:T(8,128)} %copy-done.7) | copy-start | bytes 1572868
  183.7 226.3 %copy-start.4 = (f32[512,128]{0,1:T(8,128)S(1)}, f32[512,128]{0,1:T(8,128)}, u32[]{:S(2)}) copy-start(f32[512,128]{0,1:T(8,128)} %copy-done.3) | copy-start | bytes 786436
  183.7 226.3 %copy-start.10 = (f32[2,128,512]{1,2,0:T(8,128)S(1)}, f32[2,128,512]{1,2,0:T(8,128)}, u32[]{:S(2)}) copy-start(f32[2,128,512]{1,2,0:T(8,128)} %copy-done.9) | copy-start | bytes 1572868
  183.7 227.0 %copy-start.12 = (f32[2,128,512]{1,2,0:T(8,128)S(1)}, f32[2,128,512]{1,2,0:T(8,128)}, u32[]{:S(2)}) copy-start(f32[2,128,512]{1,2,0:T(8,128)} %copy-done.11) | copy-start | bytes 1572868
  409.9 27.0 %copy-start.6 = (f32[2,128,512]{1,2,0:T(8,128)S(1)}, f32[2,128,512]{1,2,0:T(8,128)}, u32[]{:S(2)}) copy-start(f32[2,128,512]{1,2,0:T(8,128)} %copy-done.5) | copy-start | bytes 1572868
  413.4 32.1 %all-to-all-start.1 = ((f32[32,1,1024]{2,1,0:T(1,128)}), f32[32,1,1024]{2,1,0:T(1,128)S(1)}, u32[]{:S(2)}, u32[]{:S(2)}) async-start(f32[32,1,1024]{2,1,0:T(1,128)} %copy.125), calls=%async_computation.1 | async-start | bytes 262144 | tf_op jit(solution)/shard_map/all_to_all | solution.py:47
Sparse Core Ops, SparseCore 0:
  26.9 93.0 all-gather.2
  183.8 132.4 reduce-scatter.3
